TPU v7x, 32 devices: a whole 2x2x4 slice. The times are simulated.
32 devices in a mesh: parts: 2 (over y), col: 16 (over z, x, core).
Axes of the slice: x: 2, y: 2, z: 4, core: 2. Of those that a mesh axis runs over, the one named last changes fastest.
Arguments:
- alignment_rows: bfloat16 [128, 128, 256], P('parts', 'col'), parts along dimension 0, may hold values from -6 to 6
- alignment_columns: bfloat16 [128, 256, 256], P('parts', 'col'), parts along dimension 0, may hold values from -6 to 6
- slab_alignment_mask: int32 [128, 128], P('parts'), parts along dimension 0, may hold values 0 or 1
- slab_crop_mask: int32 [256], P('parts'), parts along dimension 0, may hold values 0 or 1
- column_alignment_mask: int32 [128, 256], P('parts', 'col'), parts along dimension 0, may hold values 0 or 1
- column_crop_mask: int32 [512], P(('parts', 'col')), parts along dimension 0, may hold values 0 or 1
- norm_scale_gain: float32 [256], replicated, may hold values from 0.25 to 1.75
- norm_offset_bias: float32 [256], replicated, may hold values from -3 to 3
- left_projection_weight: bfloat16 [256, 32], replicated, may hold values from -0.375 to 0.375
- right_projection_weight: bfloat16 [256, 32], replicated, may hold values from -0.375 to 0.375
- pair_output_weight: bfloat16 [1024, 128], replicated, may hold values from -1.5 to 1.5
- pair_output_bias: float32 [128], replicated, may hold values from -3 to 3
- pair_update_gradient: bfloat16 [256, 256, 128], P('parts', 'col'), parts along dimension 0, may hold values from -4 to 4
Outputs:
- pair_out: bfloat16 [256, 256, 128], P('parts', 'col'), parts along dimension 0
- grad_rows: bfloat16 [128, 128, 256], P('parts', 'col'), parts along dimension 0
- grad_cols: bfloat16 [128, 256, 256], P('parts', 'col'), parts along dimension 0
- grad_pair_weight: float32 [2048, 128], P(('parts', 'col')), parts along dimension 0
- grad_proj: float32 [512, 64], P(('parts', 'col')), parts along dimension 0
There are 2 independent parts, one for each index of `parts`. A program takes and returns all parts, laid end to end along the dimension named above; an argument that names none is the same for every part. Nothing has to cross between parts.
All inputs are finite; a program needn't handle non-finite values. No bound on the sum of `column_alignment_mask` or of `column_crop_mask` on one device may be relied on, other than what follows from the above.
Results may differ from a plain program's by a relative error of at most 0.007.
Values may be sent and summed in bfloat16 or wider, within the bound.
A program may use at most 128 MiB of HBM per device.

v0:
```python
import jax
import jax.numpy as jnp
from jax import lax
from jax.sharding import PartitionSpec as P

ALIGNMENT_WIDTH = 256
PROJECTED_WIDTH = 32
PAIR_WIDTH = 128
ALIGNMENT_COUNT = 64
SLAB_ROW_COUNT = 128
COLUMN_RESIDUES = 16
norm_eps = 1e-05
row_block_inputs = 64


def apply_layer_norm(value_array, gain, shift):
    value_array = value_array.astype(jnp.float32)
    center = value_array - jnp.mean(value_array, axis=-1, keepdims=True)
    spread = jnp.mean(center * center, axis=-1, keepdims=True)
    return center * lax.rsqrt(spread + norm_eps) * gain + shift


def per_device(
    alignment_rows,
    alignment_columns,
    slab_alignment_mask,
    slab_crop_mask,
    column_alignment_mask,
    column_crop_mask,
    norm_scale_gain,
    norm_offset_bias,
    left_projection_weight,
    right_projection_weight,
    pair_output_weight,
    pair_output_bias,
    pair_update_gradient,
):
    local_rows = alignment_rows.shape[1]
    position = lax.axis_index("col")
    row_mask_weight = (slab_alignment_mask * slab_crop_mask[None, :]).astype(jnp.float32)
    local_mask_weight = lax.dynamic_slice_in_dim(
        row_mask_weight, position * local_rows, local_rows, 1
    )
    column_mask_weight = (column_alignment_mask * column_crop_mask[None, :]).astype(jnp.float32)
    normalized_rows = apply_layer_norm(alignment_rows, norm_scale_gain, norm_offset_bias).astype(
        jnp.bfloat16
    )
    normalized_columns = apply_layer_norm(
        alignment_columns, norm_scale_gain, norm_offset_bias
    ).astype(jnp.bfloat16)
    left_local_factor = jnp.dot(
        normalized_rows.reshape(-1, ALIGNMENT_WIDTH),
        left_projection_weight,
        preferred_element_type=jnp.float32,
    )
    left_local_factor = (
        left_local_factor.reshape(ALIGNMENT_COUNT, local_rows, PROJECTED_WIDTH)
        * local_mask_weight[:, :, None]
    ).astype(jnp.bfloat16)
    left_outgoing = left_local_factor.transpose(1, 0, 2).reshape(
        local_rows, ALIGNMENT_COUNT * PROJECTED_WIDTH
    )
    right_factor = jnp.dot(
        normalized_columns.reshape(-1, ALIGNMENT_WIDTH),
        right_projection_weight,
        preferred_element_type=jnp.float32,
    )
    right_factor = (
        right_factor.reshape(ALIGNMENT_COUNT, COLUMN_RESIDUES, PROJECTED_WIDTH)
        * column_mask_weight[:, :, None]
    ).astype(jnp.bfloat16)
    denom = jnp.maximum(
        jnp.dot(
            row_mask_weight.T,
            column_mask_weight,
            precision=lax.Precision.HIGHEST,
            preferred_element_type=jnp.float32,
        ),
        1.0,
    )
    weight_back = pair_output_weight.T

    def outer_rows(remaining_rows, rows_denom):
        outer = (
            jnp.einsum(
                "isc,sjd->ijcd", remaining_rows, right_factor, preferred_element_type=jnp.float32
            )
            / rows_denom[:, :, None, None]
        )
        return outer.astype(jnp.bfloat16).reshape(-1, PROJECTED_WIDTH * PROJECTED_WIDTH)

    def outer_grad(rows_grad, rows_denom, row_inputs):
        grad_flat = rows_grad.reshape(-1, PAIR_WIDTH)
        grad_outer = (
            jnp.dot(grad_flat, weight_back, preferred_element_type=jnp.float32)
            / rows_denom.reshape(-1, 1)
        ).astype(jnp.bfloat16)
        return (
            grad_flat,
            grad_outer.reshape(row_inputs, COLUMN_RESIDUES, PROJECTED_WIDTH, PROJECTED_WIDTH),
        )

    def make_step():

        def step(carry, item):
            weight_sum, right_sum = carry
            remaining_rows, rows_denom, rows_grad = item
            flat = outer_rows(remaining_rows, rows_denom)
            grad_flat, grad_four = outer_grad(rows_grad, rows_denom, row_block_inputs)
            weight_sum = weight_sum + jnp.einsum(
                "nc,np->cp", flat, grad_flat, preferred_element_type=jnp.float32
            )
            right_sum = right_sum + jnp.einsum(
                "ijcd,isc->sjd", grad_four, remaining_rows, preferred_element_type=jnp.float32
            )
            extra = ()
            extra = extra + (
                jnp.einsum(
                    "ijcd,sjd->isc", grad_four, right_factor, preferred_element_type=jnp.float32
                ),
            )
            return ((weight_sum, right_sum), extra)

        return step

    mask_count_total = SLAB_ROW_COUNT // row_block_inputs
    denom_blocks = denom.reshape(mask_count_total, row_block_inputs, COLUMN_RESIDUES)
    grad_blocks = pair_update_gradient.reshape(
        mask_count_total, row_block_inputs, COLUMN_RESIDUES, PAIR_WIDTH
    )
    start_index = (
        jnp.zeros((PROJECTED_WIDTH * PROJECTED_WIDTH, PAIR_WIDTH), jnp.float32),
        jnp.zeros((ALIGNMENT_COUNT, COLUMN_RESIDUES, PROJECTED_WIDTH), jnp.float32),
    )
    current_piece = lax.all_gather(left_outgoing, "col", axis=0, tiled=True)
    row_inputs = current_piece.shape[0]
    remaining_rows = current_piece.reshape(row_inputs, ALIGNMENT_COUNT, PROJECTED_WIDTH)
    rows_denom = denom
    pair = (
        jnp.dot(
            outer_rows(remaining_rows, rows_denom),
            pair_output_weight,
            preferred_element_type=jnp.float32,
        )
        + pair_output_bias
    )
    pair_out = pair.astype(jnp.bfloat16).reshape(row_inputs, COLUMN_RESIDUES, PAIR_WIDTH)
    collected_blocks = lax.all_gather(left_outgoing, "col", axis=0, tiled=True)
    left_factor_blocks = collected_blocks.reshape(
        mask_count_total, row_block_inputs, ALIGNMENT_COUNT, PROJECTED_WIDTH
    )
    (weight_sum, right_sum), step_outputs = lax.scan(
        make_step(), start_index, (left_factor_blocks, denom_blocks, grad_blocks)
    )
    left_product_terms = step_outputs[0].reshape(SLAB_ROW_COUNT, ALIGNMENT_COUNT * PROJECTED_WIDTH)
    left_total_sum = lax.psum_scatter(left_product_terms, "col", scatter_dimension=0, tiled=True)
    left_total_sum = left_total_sum.reshape(local_rows, ALIGNMENT_COUNT, PROJECTED_WIDTH).transpose(
        1, 0, 2
    )
    left_side_gradient = (left_total_sum * local_mask_weight[:, :, None]).astype(jnp.bfloat16)
    right_side_gradient = (right_sum * column_mask_weight[:, :, None]).astype(jnp.bfloat16)
    projected_left = jnp.einsum(
        "nm,nc->mc",
        normalized_rows.reshape(-1, ALIGNMENT_WIDTH),
        left_side_gradient.reshape(-1, PROJECTED_WIDTH),
        preferred_element_type=jnp.float32,
    )
    projected_right = jnp.einsum(
        "nm,nc->mc",
        normalized_columns.reshape(-1, ALIGNMENT_WIDTH),
        right_side_gradient.reshape(-1, PROJECTED_WIDTH),
        preferred_element_type=jnp.float32,
    )
    proj_terms = jnp.concatenate([projected_left, projected_right], axis=1)
    grad_pair_weight, grad_proj = (
        lax.psum_scatter(weight_sum, "col", scatter_dimension=0, tiled=True),
        lax.psum_scatter(proj_terms, "col", scatter_dimension=0, tiled=True),
    )
    normalized_row_gradient = jnp.dot(
        left_side_gradient.reshape(-1, PROJECTED_WIDTH),
        left_projection_weight.T,
        preferred_element_type=jnp.float32,
    ).reshape(ALIGNMENT_COUNT, local_rows, ALIGNMENT_WIDTH)
    normalized_column_gradient = jnp.dot(
        right_side_gradient.reshape(-1, PROJECTED_WIDTH),
        right_projection_weight.T,
        preferred_element_type=jnp.float32,
    ).reshape(ALIGNMENT_COUNT, COLUMN_RESIDUES, ALIGNMENT_WIDTH)
    unused_result, row_back_grads = jax.vjp(
        lambda value_array: apply_layer_norm(value_array, norm_scale_gain, norm_offset_bias),
        alignment_rows.astype(jnp.float32),
    )
    unused_result, column_back_grads = jax.vjp(
        lambda value_array: apply_layer_norm(value_array, norm_scale_gain, norm_offset_bias),
        alignment_columns.astype(jnp.float32),
    )
    grad_rows = row_back_grads(normalized_row_gradient)[0].astype(jnp.bfloat16)
    grad_cols = column_back_grads(normalized_column_gradient)[0].astype(jnp.bfloat16)
    return (pair_out, grad_rows, grad_cols, grad_pair_weight, grad_proj)


def solution(mesh):
    placed = (
        P("parts", "col", None),
        P("parts", "col", None),
        P("parts", None),
        P("parts"),
        P("parts", "col"),
        P(("parts", "col")),
        P(),
        P(),
        P(),
        P(),
        P(),
        P(),
        P("parts", "col", None),
    )
    return jax.shard_map(
        per_device,
        mesh=mesh,
        in_specs=placed,
        out_specs=(
            P("parts", "col", None),
            P("parts", "col", None),
            P("parts", "col", None),
            P(("parts", "col"), None),
            P(("parts", "col"), None),
        ),
        check_vma=False,
    )
```

profile of v0, /device:TPU:0, one launch (start us, length us, event | category | flops | bytes accessed | tf_op | source)
XLA Modules:
  0.0 399.0 jit_solution(2750851517956724560)
XLA Ops:
  7.3 0.9 multiply_convert_fusion.4
  8.3 0.8 multiply_convert_fusion.3
  9.9 1.1 convert_reduce_fusion.1
  11.0 1.2 fusion.35
  12.2 1.3 convert_reduce_fusion
  13.5 1.4 fusion.26
  15.5 1.3 fusion.25
  17.6 0.9 copy.110
  18.5 0.8 copy.108
  19.4 24.6 %all_gather.4 = bf16[128,2048]{1,0:T(8,128)(2,1)S(1)} all-gather(bf16[8,2048]{1,0:T(8,128)(2,1)S(1)} %reshape.128), channel_id=1, replica_groups=mesh['parts'=2,'col'=16] {'col'}, dimensions={0}, use_global_device_ids=true | all-gather | bytes 557056 | tf_op jit(solution)/shard_map/all_gather | solution.py:135
  44.7 2.3 copy.109
  47.0 168.8 %while.15 = (s32[]{:T(128)}, f32[1024,128]{1,0:T(8,128)S(1)}, f32[64,16,32]{0,2,1:T(8,128)}, f32[2,64,64,32]{1,0,3,2:T(2,128)}, bf16[2,64,64,32]{2,1,3,0:T(8,128...) while((s32[]{:T(128)}, f32[1024,128]{1,0:T(8,128)S(1)}, ...), condition=%wide.region_5.6_spmd.clone, body=%wide.region_4.5_spmd.clone.sunk | while | flops 944046080 | bytes 43880792 | solution.py:152
  47.4 3.1 divide_convert_fusion.3
  50.5 3.3 fusion.90
  53.7 13.4 %copy.160 = bf16[64,16,32,32]{3,2,1,0:T(8,128)(2,1)} copy(bf16[64,16,32,32]{0,3,1,2:T(8,128)(2,1)} %fusion.90) | data formatting | bytes 4194304 | tf_op jit(solution)/shard_map/while/body/eval_jaxpr/convert_element_type | solution.py:90
  67.1 11.3 %reshape.156 = bf16[1024,1024]{1,0:T(8,128)(2,1)S(1)} reshape(bf16[64,16,32,32]{3,2,1,0:T(8,128)(2,1)} %copy.160) | data formatting | bytes 4194304 | tf_op jit(solution)/shard_map/while/body/eval_jaxpr/reshape | solution.py:90
  78.4 0.8 convolution_add_fusion.3
  79.3 11.1 %reshape.157 = bf16[64,16,32,32]{3,2,1,0:T(8,128)(2,1)} reshape(bf16[1024,1024]{1,0:T(8,128)(2,1)} %divide_convert_fusion.3) | data formatting | bytes 4194304 | tf_op jit(solution)/shard_map/while/body/eval_jaxpr/reshape | solution.py:100
  90.4 13.0 %fusion.91 = f32[64,16,32]{0,2,1:T(8,128)S(1)} fusion(bf16[64,16,32,32]{3,2,1,0:T(8,128)(2,1)} %reshape.157, bf16[2,64,64,32]{2,1,3,0:T(8,128)(2,1)S(1)} %copy-done.10, s32[]{:T(128)S(6)} %copy.168, f32[64,16,32]{0,2,1:T(8,128)S(1)} %copy-done.25, pred[]{:T(512)S(6)} %compare.3), kind=kOutput, calls=%fused_computation.8.clone.1 | convolution fusion | flops 134283264 | bytes 3014661 | tf_op jit(solution)/shard_map/while/body/eval_jaxpr/ijcd,isc->sjd/dot_general | solution.py:113
  103.5 1.7 convolution_bitcast_fusion.5
  105.2 0.8 copy.162
  106.0 25.5 %dynamic_update_slice.6 = f32[2,64,64,32]{1,0,3,2:T(2,128)} dynamic-update-slice(f32[2,64,64,32]{1,0,3,2:T(2,128)} %get-tuple-element.248, f32[1,64,64,32]{1,0,3,2:T(1,128)S(1)} %copy.162, s32[]{:T(128)S(6)} %copy.168, s32[]{:T(128)} %constant.21.clone.1..sunk, s32[]{:T(128)} %constant.21.clone.1..sunk, s32[]{:T(128)} %constant.21.clone.1..sunk) | dynamic-update-slice | bytes 1048580 | tf_op jit(solution)/shard_map/while/body/jit(dynamic_update_index_in_dim)/dynamic_update_slice | solution.py:152
  131.7 3.1 divide_convert_fusion.3
  134.8 3.3 fusion.90
  138.0 13.4 %copy.160 = bf16[64,16,32,32]{3,2,1,0:T(8,128)(2,1)} copy(bf16[64,16,32,32]{0,3,1,2:T(8,128)(2,1)} %fusion.90) | data formatting | bytes 4194304 | tf_op jit(solution)/shard_map/while/body/eval_jaxpr/convert_element_type | solution.py:90
  151.4 11.3 %reshape.156 = bf16[1024,1024]{1,0:T(8,128)(2,1)S(1)} reshape(bf16[64,16,32,32]{3,2,1,0:T(8,128)(2,1)} %copy.160) | data formatting | bytes 4194304 | tf_op jit(solution)/shard_map/while/body/eval_jaxpr/reshape | solution.py:90
  162.7 0.8 convolution_add_fusion.3
  163.6 11.1 %reshape.157 = bf16[64,16,32,32]{3,2,1,0:T(8,128)(2,1)} reshape(bf16[1024,1024]{1,0:T(8,128)(2,1)} %divide_convert_fusion.3) | data formatting | bytes 4194304 | tf_op jit(solution)/shard_map/while/body/eval_jaxpr/reshape | solution.py:100
  174.7 13.0 %fusion.91 = f32[64,16,32]{0,2,1:T(8,128)S(1)} fusion(bf16[64,16,32,32]{3,2,1,0:T(8,128)(2,1)} %reshape.157, bf16[2,64,64,32]{2,1,3,0:T(8,128)(2,1)S(1)} %copy-done.10, s32[]{:T(128)S(6)} %copy.168, f32[64,16,32]{0,2,1:T(8,128)S(1)} %copy-done.25, pred[]{:T(512)S(6)} %compare.3), kind=kOutput, calls=%fused_computation.8.clone.1 | convolution fusion | flops 134283264 | bytes 3014661 | tf_op jit(solution)/shard_map/while/body/eval_jaxpr/ijcd,isc->sjd/dot_general | solution.py:113
  187.8 1.7 convolution_bitcast_fusion.5
  189.5 0.8 copy.162
  190.3 25.5 %dynamic_update_slice.6 = f32[2,64,64,32]{1,0,3,2:T(2,128)} dynamic-update-slice(f32[2,64,64,32]{1,0,3,2:T(2,128)} %get-tuple-element.248, f32[1,64,64,32]{1,0,3,2:T(1,128)S(1)} %copy.162, s32[]{:T(128)S(6)} %copy.168, s32[]{:T(128)} %constant.21.clone.1..sunk, s32[]{:T(128)} %constant.21.clone.1..sunk, s32[]{:T(128)} %constant.21.clone.1..sunk) | dynamic-update-slice | bytes 1048580 | tf_op jit(solution)/shard_map/while/body/jit(dynamic_update_index_in_dim)/dynamic_update_slice | solution.py:152
  215.8 2.8 reshape.135
  218.7 1.3 copy.128
  220.1 0.7 reduce-scatter.8.cloned.1.call-update
  221.3 0.8 convolution_bitcast_fusion.2
  222.7 0.6 fusion.42
  223.4 1.4 add_convert_fusion
  224.8 3.2 fusion.17
  228.0 23.0 %copy.106 = bf16[128,16,32,32]{3,2,1,0:T(8,128)(2,1)} copy(bf16[128,16,32,32]{0,3,2,1:T(8,128)(2,1)} %fusion.17) | data formatting | bytes 8388608 | tf_op jit(solution)/shard_map/convert_element_type | solution.py:90
  251.1 23.3 %reshape.130 = bf16[2048,1024]{1,0:T(8,128)(2,1)} reshape(bf16[128,16,32,32]{3,2,1,0:T(8,128)(2,1)} %copy.106) | data formatting | bytes 8388608 | tf_op jit(solution)/shard_map/reshape | solution.py:90
  274.4 4.3 %fusion.18 = bf16[2048,128]{1,0:T(8,128)(2,1)} fusion(bf16[2048,1024]{1,0:T(8,128)(2,1)} %reshape.130, bf16[1024,128]{1,0:T(8,128)(2,1)S(1)} %copy-done.31, f32[128]{0:T(128)S(1)} %copy-done.43), kind=kOutput, calls=%fused_computation.22 | convolution fusion | flops 537395200 | bytes 4981248 | tf_op jit(solution)/shard_map/dot_general | solution.py:140
  278.7 1.2 copy.129
  279.9 0.6 copy.114
  281.1 0.8 copy.130
  282.6 1.0 add_convert_fusion.1
  283.6 50.7 %reduce-scatter.8.cloned.1.call-done = f32[64,128]{1,0:T(8,128)} async-done(((f32[1024,128]{1,0:T(8,128)}), f32[64,128]{1,0:T(8,128)}) %reduce-scatter.8.cloned.1.call-update) | async-done | bytes 32784 | tf_op jit(solution)/shard_map/reduce_scatter | solution.py:176
  334.3 58.2 %reduce-scatter.12.cloned.1.call-done = f32[16,64]{1,0:T(8,128)} async-done(((f32[256,64]{1,0:T(8,128)}), f32[16,64]{1,0:T(8,128)}) %reduce-scatter.12.cloned.1.call-update) | async-done | bytes 4112
  (146 shorter events, 5.8 us)
Async XLA Ops:
  7.2 9.9 %copy-start = (bf16[256,32]{0,1:T(8,128)(2,1)S(1)}, bf16[256,32]{0,1:T(8,128)(2,1)}, u32[]{:S(2)}) copy-start(bf16[256,32]{0,1:T(8,128)(2,1)} %param.24) | copy-start | bytes 49156
  7.2 9.9 %copy-start.3 = (bf16[64,16,256]{2,1,0:T(8,128)(2,1)S(1)}, bf16[64,16,256]{2,1,0:T(8,128)(2,1)}, u32[]{:S(2)}) copy-start(bf16[64,16,256]{2,1,0:T(8,128)(2,1)} %param.16) | copy-start | bytes 1572868
  7.2 9.9 %copy-start.39 = (f32[256]{0:T(256)S(1)}, f32[256]{0:T(256)}, u32[]{:S(2)}) copy-start(f32[256]{0:T(256)} %param.21) | copy-start | bytes 3076
  7.2 9.9 %copy-start.41 = (f32[256]{0:T(256)S(1)}, f32[256]{0:T(256)}, u32[]{:S(2)}) copy-start(f32[256]{0:T(256)} %param.22) | copy-start | bytes 3076
  7.2 11.3 %copy-start.30 = (bf16[1024,128]{1,0:T(8,128)(2,1)S(1)}, bf16[1024,128]{1,0:T(8,128)(2,1)}, u32[]{:S(2)}) copy-start(bf16[1024,128]{1,0:T(8,128)(2,1)} %param.25) | copy-start | bytes 786436
  7.2 271.5 %reduce-scatter.10.cloned.1.call-start = ((), (), s32[]{:S(2)}) async-start(), calls=%async_computation.4 | async-start | bytes 1114112
  8.3 36.0 %copy-start.32 = (f32[64,16]{1,0:T(8,128)}, f32[64,16]{1,0:T(8,128)S(1)}, u32[]{:S(2)}) copy-start(f32[64,16]{1,0:T(8,128)S(1)} %copy.101) | copy-start | bytes 12292
  11.0 32.9 %copy-start.13 = (f32[64,8]{1,0:T(8,128)}, f32[64,8]{1,0:T(8,128)S(1)}, u32[]{:S(2)}) copy-start(f32[64,8]{1,0:T(8,128)S(1)} %broadcast_multiply_fusion) | copy-start | bytes 6148
  12.2 31.7 %copy-start.19 = (f32[64,8]{1,0:T(8,128)}, f32[64,8]{1,0:T(8,128)S(1)}, u32[]{:S(2)}) copy-start(f32[64,8]{1,0:T(8,128)S(1)} %fusion.35) | copy-start | bytes 6148
  12.2 31.7 %copy-start.17 = (f32[64,8]{1,0:T(8,128)}, f32[64,8]{1,0:T(8,128)S(1)}, u32[]{:S(2)}) copy-start(f32[64,8]{1,0:T(8,128)S(1)} %fusion.51) | copy-start | bytes 6148
  13.5 31.1 %copy-start.11 = (f32[64,16]{1,0:T(8,128)}, f32[64,16]{1,0:T(8,128)S(1)}, u32[]{:S(2)}) copy-start(f32[64,16]{1,0:T(8,128)S(1)} %broadcast_multiply_fusion.1) | copy-start | bytes 12292
  15.5 31.4 %copy-start.21 = (f32[64,16]{1,0:T(8,128)}, f32[64,16]{1,0:T(8,128)S(1)}, u32[]{:S(2)}) copy-start(f32[64,16]{1,0:T(8,128)S(1)} %fusion.50) | copy-start | bytes 12292
  16.9 30.1 %copy-start.6 = (bf16[128,16,128]{2,1,0:T(8,128)(2,1)S(1)}, bf16[128,16,128]{2,1,0:T(8,128)(2,1)}, u32[]{:S(2)}) copy-start(bf16[128,16,128]{2,1,0:T(8,128)(2,1)} %param.27) | copy-start | bytes 1572868
  17.6 26.3 %copy-start.28 = (bf16[64,16,32]{2,1,0:T(8,128)(2,1)}, bf16[64,16,32]{2,1,0:T(8,128)(2,1)S(1)}, u32[]{:S(2)}) copy-start(bf16[64,16,32]{2,1,0:T(8,128)(2,1)S(1)} %fusion.23) | copy-start | bytes 196612
  47.4 3.1 copy-start.9
  47.4 3.1 copy-start.34
  79.3 11.1 %copy-start.10 = (bf16[2,64,64,32]{2,1,3,0:T(8,128)(2,1)S(1)}, bf16[2,64,64,32]{2,1,3,0:T(8,128)(2,1)}, u32[]{:S(2)}) copy-start(bf16[2,64,64,32]{2,1,3,0:T(8,128)(2,1)} %get-tuple-element.260) | copy-start | bytes 1572868 | tf_op jit(solution)/shard_map/while
  79.3 11.1 %copy-start.25 = (f32[64,16,32]{0,2,1:T(8,128)S(1)}, f32[64,16,32]{0,2,1:T(8,128)}, u32[]{:S(2)}) copy-start(f32[64,16,32]{0,2,1:T(8,128)} %get-tuple-element.247) | copy-start | bytes 393220 | tf_op jit(solution)/shard_map/while
  90.4 13.1 %copy-start.1 = (bf16[64,16,32,32]{3,2,1,0:T(8,128)(2,1)S(1)}, bf16[64,16,32,32]{3,2,1,0:T(8,128)(2,1)}, u32[]{:S(2)}) copy-start(bf16[64,16,32,32]{3,2,1,0:T(8,128)(2,1)} %reshape.157) | copy-start | bytes 6291460 | tf_op jit(solution)/shard_map/while
  90.4 13.1 %copy-start.35 = (bf16[64,16,32]{0,2,1:T(8,128)(2,1)S(1)}, bf16[64,16,32]{0,2,1:T(8,128)(2,1)}, u32[]{:S(2)}) copy-start(bf16[64,16,32]{0,2,1:T(8,128)(2,1)} %get-tuple-element.261) | copy-start | bytes 196612 | tf_op jit(solution)/shard_map/while
  131.7 3.1 copy-start.9
  131.7 3.1 copy-start.34
  163.6 11.1 %copy-start.10 = (bf16[2,64,64,32]{2,1,3,0:T(8,128)(2,1)S(1)}, bf16[2,64,64,32]{2,1,3,0:T(8,128)(2,1)}, u32[]{:S(2)}) copy-start(bf16[2,64,64,32]{2,1,3,0:T(8,128)(2,1)} %get-tuple-element.260) | copy-start | bytes 1572868 | tf_op jit(solution)/shard_map/while
  163.6 11.1 %copy-start.25 = (f32[64,16,32]{0,2,1:T(8,128)S(1)}, f32[64,16,32]{0,2,1:T(8,128)}, u32[]{:S(2)}) copy-start(f32[64,16,32]{0,2,1:T(8,128)} %get-tuple-element.247) | copy-start | bytes 393220 | tf_op jit(solution)/shard_map/while
  174.7 13.1 %copy-start.1 = (bf16[64,16,32,32]{3,2,1,0:T(8,128)(2,1)S(1)}, bf16[64,16,32,32]{3,2,1,0:T(8,128)(2,1)}, u32[]{:S(2)}) copy-start(bf16[64,16,32,32]{3,2,1,0:T(8,128)(2,1)} %reshape.157) | copy-start | bytes 6291460 | tf_op jit(solution)/shard_map/while
  174.7 13.1 %copy-start.35 = (bf16[64,16,32]{0,2,1:T(8,128)(2,1)S(1)}, bf16[64,16,32]{0,2,1:T(8,128)(2,1)}, u32[]{:S(2)}) copy-start(bf16[64,16,32]{0,2,1:T(8,128)(2,1)} %get-tuple-element.261) | copy-start | bytes 196612 | tf_op jit(solution)/shard_map/while
  215.8 4.3 %copy-start.2 = (f32[1024,128]{1,0:T(8,128)}, f32[1024,128]{1,0:T(8,128)S(1)}, u32[]{:S(2)}) copy-start(f32[1024,128]{1,0:T(8,128)S(1)} %get-tuple-element.56) | copy-start | bytes 1572868
  215.8 5.1 %copy-start.16 = (f32[64,128]{1,0:T(8,128)S(1)}, f32[64,128]{1,0:T(8,128)}, u32[]{:S(2)}) copy-start(f32[64,128]{1,0:T(8,128)} %copy-done.15) | copy-start | bytes 98308
  215.8 5.2 %copy-start.27 = (f32[64,16,32]{0,2,1:T(8,128)S(1)}, f32[64,16,32]{0,2,1:T(8,128)}, u32[]{:S(2)}) copy-start(f32[64,16,32]{0,2,1:T(8,128)} %get-tuple-element.55) | copy-start | bytes 393220
  215.8 5.5 %copy-start.4 = (bf16[64,16,256]{2,1,0:T(8,128)(2,1)S(1)}, bf16[64,16,256]{2,1,0:T(8,128)(2,1)}, u32[]{:S(2)}) copy-start(bf16[64,16,256]{2,1,0:T(8,128)(2,1)} %param.16) | copy-start | bytes 1572868
  215.8 5.4 %copy-start.12 = (f32[64,16]{1,0:T(8,128)S(1)}, f32[64,16]{1,0:T(8,128)}, u32[]{:S(2)}) copy-start(f32[64,16]{1,0:T(8,128)} %copy-done.11) | copy-start | bytes 12292
  215.8 5.4 %copy-start.22 = (f32[64,16]{1,0:T(8,128)S(1)}, f32[64,16]{1,0:T(8,128)}, u32[]{:S(2)}) copy-start(f32[64,16]{1,0:T(8,128)} %copy-done.21) | copy-start | bytes 12292
  215.8 5.4 %copy-start.33 = (f32[64,16]{1,0:T(8,128)S(1)}, f32[64,16]{1,0:T(8,128)}, u32[]{:S(2)}) copy-start(f32[64,16]{1,0:T(8,128)} %copy-done.32) | copy-start | bytes 12292
  215.8 5.4 %copy-start.40 = (f32[256]{0:T(256)S(1)}, f32[256]{0:T(256)}, u32[]{:S(2)}) copy-start(f32[256]{0:T(256)} %param.21) | copy-start | bytes 3076
  215.8 5.4 %copy-start.42 = (f32[256]{0:T(256)S(1)}, f32[256]{0:T(256)}, u32[]{:S(2)}) copy-start(f32[256]{0:T(256)} %param.22) | copy-start | bytes 3076
  218.7 4.0 %copy-start.24 = (f32[64,16]{1,0:T(8,128)S(1)}, f32[64,16]{1,0:T(8,128)}, u32[]{:S(2)}) copy-start(f32[64,16]{1,0:T(8,128)} %copy-done.23) | copy-start | bytes 12292
  220.0 114.3 %reduce-scatter.8.cloned.1.call-start = ((), (), s32[]{:S(2)}) async-start(), calls=%async_computation.3 | async-start | bytes 557056 | tf_op jit(solution)/shard_map/reduce_scatter | solution.py:176
  220.8 171.7 %reduce-scatter.12.cloned.1.call-start = ((), (), s32[]{:S(2)}) async-start(), calls=%async_computation.5 | async-start | bytes 139264
  221.3 3.5 copy-start.8
  221.3 3.5 copy-start.29
  221.3 3.5 copy-start.37
  251.1 23.3 %copy-start.31 = (bf16[1024,128]{1,0:T(8,128)(2,1)S(1)}, bf16[1024,128]{1,0:T(8,128)(2,1)}, u32[]{:S(2)}) copy-start(bf16[1024,128]{1,0:T(8,128)(2,1)} %param.25) | copy-start | bytes 786436
  251.1 23.3 %copy-start.43 = (f32[128]{0:T(128)S(1)}, f32[128]{0:T(128)}, u32[]{:S(2)}) copy-start(f32[128]{0:T(128)} %param.26) | copy-start | bytes 1540
  274.4 6.3 %copy-start.5 = (bf16[64,8,256]{2,1,0:T(8,128)(2,1)S(1)}, bf16[64,8,256]{2,1,0:T(8,128)(2,1)}, u32[]{:S(2)}) copy-start(bf16[64,8,256]{2,1,0:T(8,128)(2,1)} %param.15) | copy-start | bytes 786436
  274.4 6.3 %copy-start.14 = (f32[64,8]{1,0:T(8,128)S(1)}, f32[64,8]{1,0:T(8,128)}, u32[]{:S(2)}) copy-start(f32[64,8]{1,0:T(8,128)} %copy-done.13) | copy-start | bytes 6148
  274.4 6.3 %copy-start.18 = (f32[64,8]{1,0:T(8,128)S(1)}, f32[64,8]{1,0:T(8,128)}, u32[]{:S(2)}) copy-start(f32[64,8]{1,0:T(8,128)} %copy-done.17) | copy-start | bytes 6148
  274.4 7.4 %copy-start.38 = (bf16[256,32]{0,1:T(8,128)(2,1)S(1)}, bf16[256,32]{0,1:T(8,128)(2,1)}, u32[]{:S(2)}) copy-start(bf16[256,32]{0,1:T(8,128)(2,1)} %param.23) | copy-start | bytes 49156
  274.4 7.7 %copy-start.20 = (f32[64,8]{1,0:T(8,128)S(1)}, f32[64,8]{1,0:T(8,128)}, u32[]{:S(2)}) copy-start(f32[64,8]{1,0:T(8,128)} %copy-done.19) | copy-start | bytes 6148
  (6 other events, 8.2 us)
Sparse Core Ops, SparseCore 0:
  220.2 54.6 reduce-scatter.9
  279.4 54.8 reduce-scatter.7
  338.4 54.0 reduce-scatter.11
where the time goes:
time: 405 us; the launch traced here: 399 us
  local copies, waits for them, and re-layouts  185 us (46%)
  waiting for transfers between devices  110 us (27%)
  matrix products  55.1 us (14%)
  blocking collectives  24.6 us (6%)
  between operations  14.4 us (4%)
  other arithmetic  10.2 us (3%)
    unnamed x5, waiting for transfers between devices  58.9 us
    dynamic_update_slice x4, local copies, waits for them, and re-layouts, per_device(): lax.scan(make_step(), start_index, (left_factor_blocks, denom_blocks, gra...  52.6 us
    reduce_scatter x1, waiting for transfers between devices, per_device(): lax.psum_scatter(weight_sum, 'col', scatter_dimension=0, tiled=True)  50.7 us
    convert_element_type x3, local copies, waits for them, and re-layouts, outer_rows(): outer.astype(jnp.bfloat16).reshape(-1, PROJECTED_WIDTH * PROJECTED_WIDTH)  49.8 us
    reshape x3, local copies, waits for them, and re-layouts, outer_rows(): outer.astype(jnp.bfloat16).reshape(-1, PROJECTED_WIDTH * PROJECTED_WIDTH)  46 us
    dot_general x2, matrix products, step(): jnp.einsum('ijcd,isc->sjd', grad_four, remaining_rows, preferred_element_...  26.1 us
    all_gather x1, blocking collectives, per_device(): current_piece = lax.all_gather(left_outgoing, 'col', axis=0, tiled=True)  24.6 us
    reshape x2, local copies, waits for them, and re-layouts, outer_grad(): grad_outer.reshape(row_inputs, COLUMN_RESIDUES, PROJECTED_WIDTH, PROJECTE...  22.2 us
  transfers between devices with their start and end apart: 3, of which 2 were waited for; matrix products, arithmetic and copies ran while one was open for 16% of the time, Pallas kernels for 0%

commit v1 on v0

--- a/solution.py
+++ b/solution.py
@@ -132,7 +132,25 @@
         jnp.zeros((PROJECTED_WIDTH * PROJECTED_WIDTH, PAIR_WIDTH), jnp.float32),
         jnp.zeros((ALIGNMENT_COUNT, COLUMN_RESIDUES, PROJECTED_WIDTH), jnp.float32),
     )
-    current_piece = lax.all_gather(left_outgoing, "col", axis=0, tiled=True)
+
+    def state_the_surface(local_x, which_axis="col"):
+        n_dev_all = jax.lax.axis_size(which_axis)
+        tray = [local_x]
+        nth = 0
+        while nth < n_dev_all - 1:
+            tray.append(
+                jax.lax.ppermute(
+                    tray[-1], which_axis, [(b, (b + 1) % n_dev_all) for b in range(n_dev_all)]
+                )
+            )
+            nth += 1
+        return jnp.roll(
+            jnp.concatenate(tray[::-1], axis=0),
+            (jax.lax.axis_index(which_axis) + 1) * local_x.shape[0],
+            axis=0,
+        )
+
+    current_piece = state_the_surface(left_outgoing)
     row_inputs = current_piece.shape[0]
     remaining_rows = current_piece.reshape(row_inputs, ALIGNMENT_COUNT, PROJECTED_WIDTH)
     rows_denom = denom

time: 405 us -> 447 us (1.10)
  waiting for transfers between devices: 110 us -> 139 us
  loops' own time: 0.46 us -> 13.3 us
  local copies, waits for them, and re-layouts: 185 us -> 180 us
    ppermute x0 -> x15, waiting for transfers between devices: none -> 87.2 us  [state_the_surface(): jax.lax.ppermute(tray[-1], which_axis, [(b, (b + 1) % n_dev_all) for b in...]
    reduce_scatter x1, waiting for transfers between devices: 50.7 us -> 0.01 us  [per_device(): lax.psum_scatter(weight_sum, 'col', scatter_dimension=0, tiled=True)]
    another operation x1, loops' own time: 0.46 us -> 13.3 us  [per_device(): lax.scan(make_step(), start_index, (left_factor_blocks, denom_blocks, gra...]
    unnamed x5, waiting for transfers between devices: 58.9 us -> 51.5 us
    reshape x2, local copies, waits for them, and re-layouts: 22.2 us -> 15.9 us  [outer_grad(): grad_outer.reshape(row_inputs, COLUMN_RESIDUES, PROJECTED_WIDTH, PROJECTE...]
    unnamed x80 -> x109, local copies, waits for them, and re-layouts: 8.57 us -> 9.77 us
  transfers between devices with their start and end apart: 3 -> 18, of which waited for: 2 -> 16; matrix products, arithmetic and copies ran while one was open for 16% -> 14% of each run, Pallas kernels for 0% -> 0%
where the time goes in v1:
time: 447 us; the launch traced here: 439 us
  local copies, waits for them, and re-layouts  180 us (40%)
  waiting for transfers between devices  139 us (31%)
  matrix products  56.8 us (13%)
  blocking collectives  24.7 us (6%)
  between operations  15 us (3%)
  loops' own time  13.3 us (3%)
  other arithmetic  10.1 us (2%)
    ppermute x15, waiting for transfers between devices, state_the_surface(): jax.lax.ppermute(tray[-1], which_axis, [(b, (b + 1) % n_dev_all) for b in...  87.2 us
    dynamic_update_slice x4, local copies, waits for them, and re-layouts, per_device(): lax.scan(make_step(), start_index, (left_factor_blocks, denom_blocks, gra...  52.6 us
    unnamed x5, waiting for transfers between devices  51.5 us
    convert_element_type x3, local copies, waits for them, and re-layouts, outer_rows(): outer.astype(jnp.bfloat16).reshape(-1, PROJECTED_WIDTH * PROJECTED_WIDTH)  49.9 us
    reshape x3, local copies, waits for them, and re-layouts, outer_rows(): outer.astype(jnp.bfloat16).reshape(-1, PROJECTED_WIDTH * PROJECTED_WIDTH)  45.9 us
    dot_general x2, matrix products, step(): jnp.einsum('ijcd,isc->sjd', grad_four, remaining_rows, preferred_element_...  26.4 us
    all_gather x1, blocking collectives, per_device(): collected_blocks = lax.all_gather(left_outgoing, 'col', axis=0, tiled=True)  24.7 us
    reshape x2, local copies, waits for them, and re-layouts, outer_grad(): grad_outer.reshape(row_inputs, COLUMN_RESIDUES, PROJECTED_WIDTH, PROJECTE...  15.9 us
  transfers between devices with their start and end apart: 18, of which 16 were waited for; matrix products, arithmetic and copies ran while one was open for 14% of the time, Pallas kernels for 0%

profile of v1, /device:TPU:0, one launch (start us, length us, event | category | flops | bytes accessed | tf_op | source)
XLA Modules:
  0.0 439.0 jit_solution(13219011288527759122)
XLA Ops:
  10.3 1.2 fusion.35
  12.7 1.3 fusion.25
  14.3 1.3 convert_reduce_fusion
  15.6 1.4 fusion.26
  17.0 24.7 %all_gather.3 = bf16[128,2048]{1,0:T(8,128)(2,1)S(1)} all-gather(bf16[8,2048]{1,0:T(8,128)(2,1)S(1)} %reshape.128), channel_id=1, replica_groups=mesh['parts'=2,'col'=16] {'col'}, dimensions={0}, use_global_device_ids=true | all-gather | bytes 557056 | tf_op jit(solution)/shard_map/all_gather | solution.py:166
  42.4 2.3 copy.109
  46.3 1.8 copy.108
  48.1 177.1 %while.15 = (s32[]{:T(128)}, f32[1024,128]{1,0:T(8,128)S(1)}, f32[64,16,32]{0,2,1:T(8,128)}, f32[2,64,64,32]{1,0,3,2:T(2,128)}, bf16[2,64,64,32]{2,1,3,0:T(8,128...) while((s32[]{:T(128)}, f32[1024,128]{1,0:T(8,128)S(1)}, ...), condition=%wide.region_5.6_spmd.clone, body=%wide.region_4.5_spmd.clone.sunk | while | flops 944046080 | bytes 45319384 | solution.py:170
  61.1 4.3 fusion.90
  65.5 13.4 %copy.160 = bf16[64,16,32,32]{3,2,1,0:T(8,128)(2,1)} copy(bf16[64,16,32,32]{0,3,1,2:T(8,128)(2,1)} %fusion.90) | data formatting | bytes 4194304 | tf_op jit(solution)/shard_map/while/body/eval_jaxpr/convert_element_type | solution.py:90
  78.9 11.3 %reshape.156 = bf16[1024,1024]{1,0:T(8,128)(2,1)S(1)} reshape(bf16[64,16,32,32]{3,2,1,0:T(8,128)(2,1)} %copy.160) | data formatting | bytes 4194304 | tf_op jit(solution)/shard_map/while/body/eval_jaxpr/reshape | solution.py:90
  91.3 1.7 divide_convert_fusion.3
  92.9 8.0 %reshape.157 = bf16[64,16,32,32]{3,2,1,0:T(8,128)(2,1)} reshape(bf16[1024,1024]{1,0:T(8,128)(2,1)S(1)} %divide_convert_fusion.3) | data formatting | bytes 4194304 | tf_op jit(solution)/shard_map/while/body/eval_jaxpr/reshape | solution.py:100
  100.9 13.2 %fusion.91 = f32[64,16,32]{0,2,1:T(8,128)S(1)} fusion(bf16[64,16,32,32]{3,2,1,0:T(8,128)(2,1)} %reshape.157, bf16[2,64,64,32]{2,1,3,0:T(8,128)(2,1)} %get-tuple-element.260, s32[]{:T(128)} %get-tuple-element.245, f32[64,16,32]{0,2,1:T(8,128)S(1)} %copy-done.23, pred[]{:T(512)S(6)} %compare.4), kind=kOutput, calls=%fused_computation.8.clone.1 | convolution fusion | flops 134283264 | bytes 9175553 | tf_op jit(solution)/shard_map/while/body/eval_jaxpr/ijcd,isc->sjd/dot_general | solution.py:113
  114.1 2.7 convolution_bitcast_fusion.5
  117.7 25.5 %dynamic_update_slice.6 = f32[2,64,64,32]{1,0,3,2:T(2,128)} dynamic-update-slice(f32[2,64,64,32]{1,0,3,2:T(2,128)} %get-tuple-element.248, f32[1,64,64,32]{1,0,3,2:T(1,128)S(1)} %copy.162, s32[]{:T(128)} %get-tuple-element.245, s32[]{:T(128)} %constant.60.clone.1..sunk, s32[]{:T(128)} %constant.60.clone.1..sunk, s32[]{:T(128)} %constant.60.clone.1..sunk) | dynamic-update-slice | bytes 1048580 | tf_op jit(solution)/shard_map/while/body/jit(dynamic_update_index_in_dim)/dynamic_update_slice | solution.py:170
  143.2 4.3 fusion.90
  147.5 13.4 %copy.160 = bf16[64,16,32,32]{3,2,1,0:T(8,128)(2,1)} copy(bf16[64,16,32,32]{0,3,1,2:T(8,128)(2,1)} %fusion.90) | data formatting | bytes 4194304 | tf_op jit(solution)/shard_map/while/body/eval_jaxpr/convert_element_type | solution.py:90
  160.9 11.3 %reshape.156 = bf16[1024,1024]{1,0:T(8,128)(2,1)S(1)} reshape(bf16[64,16,32,32]{3,2,1,0:T(8,128)(2,1)} %copy.160) | data formatting | bytes 4194304 | tf_op jit(solution)/shard_map/while/body/eval_jaxpr/reshape | solution.py:90
  173.3 1.7 divide_convert_fusion.3
  174.9 8.0 %reshape.157 = bf16[64,16,32,32]{3,2,1,0:T(8,128)(2,1)} reshape(bf16[1024,1024]{1,0:T(8,128)(2,1)S(1)} %divide_convert_fusion.3) | data formatting | bytes 4194304 | tf_op jit(solution)/shard_map/while/body/eval_jaxpr/reshape | solution.py:100
  182.9 13.2 %fusion.91 = f32[64,16,32]{0,2,1:T(8,128)S(1)} fusion(bf16[64,16,32,32]{3,2,1,0:T(8,128)(2,1)} %reshape.157, bf16[2,64,64,32]{2,1,3,0:T(8,128)(2,1)} %get-tuple-element.260, s32[]{:T(128)} %get-tuple-element.245, f32[64,16,32]{0,2,1:T(8,128)S(1)} %copy-done.23, pred[]{:T(512)S(6)} %compare.4), kind=kOutput, calls=%fused_computation.8.clone.1 | convolution fusion | flops 134283264 | bytes 9175553 | tf_op jit(solution)/shard_map/while/body/eval_jaxpr/ijcd,isc->sjd/dot_general | solution.py:113
  196.1 2.7 convolution_bitcast_fusion.5
  199.7 25.5 %dynamic_update_slice.6 = f32[2,64,64,32]{1,0,3,2:T(2,128)} dynamic-update-slice(f32[2,64,64,32]{1,0,3,2:T(2,128)} %get-tuple-element.248, f32[1,64,64,32]{1,0,3,2:T(1,128)S(1)} %copy.162, s32[]{:T(128)} %get-tuple-element.245, s32[]{:T(128)} %constant.60.clone.1..sunk, s32[]{:T(128)} %constant.60.clone.1..sunk, s32[]{:T(128)} %constant.60.clone.1..sunk) | dynamic-update-slice | bytes 1048580 | tf_op jit(solution)/shard_map/while/body/jit(dynamic_update_index_in_dim)/dynamic_update_slice | solution.py:170
  225.2 2.8 reshape.135
  228.1 1.4 copy.128
  229.9 5.7 %collective-permute-done = bf16[8,2048]{1,0:T(8,128)(2,1)S(1)} collective-permute-done((bf16[8,2048]{1,0:T(8,128)(2,1)S(1)}, bf16[8,2048]{1,0:T(8,128)(2,1)S(1)}, u32[]{:S(2)}, u32[]{:S(2)}) %collective-permute-start) | collective-permute-done | bytes 32800 | tf_op jit(solution)/shard_map/ppermute | solution.py:142
  235.6 6.0 %collective-permute-done.1 = bf16[8,2048]{1,0:T(8,128)(2,1)S(1)} collective-permute-done((bf16[8,2048]{1,0:T(8,128)(2,1)S(1)}, bf16[8,2048]{1,0:T(8,128)(2,1)S(1)}, u32[]{:S(2)}, u32[]{:S(2)}) %collective-permute-start.1) | collective-permute-done | bytes 32800 | tf_op jit(solution)/shard_map/ppermute | solution.py:142
  241.6 6.0 %collective-permute-done.2 = bf16[8,2048]{1,0:T(8,128)(2,1)S(1)} collective-permute-done((bf16[8,2048]{1,0:T(8,128)(2,1)S(1)}, bf16[8,2048]{1,0:T(8,128)(2,1)S(1)}, u32[]{:S(2)}, u32[]{:S(2)}) %collective-permute-start.2) | collective-permute-done | bytes 32800 | tf_op jit(solution)/shard_map/ppermute | solution.py:142
  247.7 6.0 %collective-permute-done.3 = bf16[8,2048]{1,0:T(8,128)(2,1)S(1)} collective-permute-done((bf16[8,2048]{1,0:T(8,128)(2,1)S(1)}, bf16[8,2048]{1,0:T(8,128)(2,1)S(1)}, u32[]{:S(2)}, u32[]{:S(2)}) %collective-permute-start.3) | collective-permute-done | bytes 32800 | tf_op jit(solution)/shard_map/ppermute | solution.py:142
  253.7 6.4 %collective-permute-done.4 = bf16[8,2048]{1,0:T(8,128)(2,1)S(1)} collective-permute-done((bf16[8,2048]{1,0:T(8,128)(2,1)S(1)}, bf16[8,2048]{1,0:T(8,128)(2,1)S(1)}, u32[]{:S(2)}, u32[]{:S(2)}) %collective-permute-start.4) | collective-permute-done | bytes 32800 | tf_op jit(solution)/shard_map/ppermute | solution.py:142
  260.1 6.1 %collective-permute-done.5 = bf16[8,2048]{1,0:T(8,128)(2,1)S(1)} collective-permute-done((bf16[8,2048]{1,0:T(8,128)(2,1)S(1)}, bf16[8,2048]{1,0:T(8,128)(2,1)S(1)}, u32[]{:S(2)}, u32[]{:S(2)}) %collective-permute-start.5) | collective-permute-done | bytes 32800 | tf_op jit(solution)/shard_map/ppermute | solution.py:142
  266.3 6.0 %collective-permute-done.6 = bf16[8,2048]{1,0:T(8,128)(2,1)S(1)} collective-permute-done((bf16[8,2048]{1,0:T(8,128)(2,1)S(1)}, bf16[8,2048]{1,0:T(8,128)(2,1)S(1)}, u32[]{:S(2)}, u32[]{:S(2)}) %collective-permute-start.6) | collective-permute-done | bytes 32800 | tf_op jit(solution)/shard_map/ppermute | solution.py:142
  272.7 5.6 %collective-permute-done.7 = bf16[8,2048]{1,0:T(8,128)(2,1)S(1)} collective-permute-done((bf16[8,2048]{1,0:T(8,128)(2,1)S(1)}, bf16[8,2048]{1,0:T(8,128)(2,1)S(1)}, u32[]{:S(2)}, u32[]{:S(2)}) %collective-permute-start.7) | collective-permute-done | bytes 32800 | tf_op jit(solution)/shard_map/ppermute | solution.py:142
  278.9 5.6 %collective-permute-done.8 = bf16[8,2048]{1,0:T(8,128)(2,1)S(1)} collective-permute-done((bf16[8,2048]{1,0:T(8,128)(2,1)S(1)}, bf16[8,2048]{1,0:T(8,128)(2,1)S(1)}, u32[]{:S(2)}, u32[]{:S(2)}) %collective-permute-start.8) | collective-permute-done | bytes 32800 | tf_op jit(solution)/shard_map/ppermute | solution.py:142
  284.5 6.0 %collective-permute-done.9 = bf16[8,2048]{1,0:T(8,128)(2,1)S(1)} collective-permute-done((bf16[8,2048]{1,0:T(8,128)(2,1)S(1)}, bf16[8,2048]{1,0:T(8,128)(2,1)S(1)}, u32[]{:S(2)}, u32[]{:S(2)}) %collective-permute-start.9) | collective-permute-done | bytes 32800 | tf_op jit(solution)/shard_map/ppermute | solution.py:142
  291.2 5.4 %collective-permute-done.10 = bf16[8,2048]{1,0:T(8,128)(2,1)S(1)} collective-permute-done((bf16[8,2048]{1,0:T(8,128)(2,1)S(1)}, bf16[8,2048]{1,0:T(8,128)(2,1)S(1)}, u32[]{:S(2)}, u32[]{:S(2)}) %collective-permute-start.10) | collective-permute-done | bytes 32800 | tf_op jit(solution)/shard_map/ppermute | solution.py:142
  296.6 6.0 %collective-permute-done.11 = bf16[8,2048]{1,0:T(8,128)(2,1)S(1)} collective-permute-done((bf16[8,2048]{1,0:T(8,128)(2,1)S(1)}, bf16[8,2048]{1,0:T(8,128)(2,1)S(1)}, u32[]{:S(2)}, u32[]{:S(2)}) %collective-permute-start.11) | collective-permute-done | bytes 32800 | tf_op jit(solution)/shard_map/ppermute | solution.py:142
  302.6 1.4 add_convert_fusion
  304.0 4.6 %collective-permute-done.12 = bf16[8,2048]{1,0:T(8,128)(2,1)S(1)} collective-permute-done((bf16[8,2048]{1,0:T(8,128)(2,1)S(1)}, bf16[8,2048]{1,0:T(8,128)(2,1)S(1)}, u32[]{:S(2)}, u32[]{:S(2)}) %collective-permute-start.12) | collective-permute-done | bytes 32800 | tf_op jit(solution)/shard_map/ppermute | solution.py:142
  309.4 5.3 %collective-permute-done.13 = bf16[8,2048]{1,0:T(8,128)(2,1)S(1)} collective-permute-done((bf16[8,2048]{1,0:T(8,128)(2,1)S(1)}, bf16[8,2048]{1,0:T(8,128)(2,1)S(1)}, u32[]{:S(2)}, u32[]{:S(2)}) %collective-permute-start.13) | collective-permute-done | bytes 32800 | tf_op jit(solution)/shard_map/ppermute | solution.py:142
  314.8 6.3 %collective-permute-done.14 = bf16[8,2048]{1,0:T(8,128)(2,1)S(1)} collective-permute-done((bf16[8,2048]{1,0:T(8,128)(2,1)S(1)}, bf16[8,2048]{1,0:T(8,128)(2,1)S(1)}, u32[]{:S(2)}, u32[]{:S(2)}) %collective-permute-start.14) | collective-permute-done | bytes 32800 | tf_op jit(solution)/shard_map/ppermute | solution.py:142
  321.8 3.2 fusion.17
  325.1 23.1 %copy.106 = bf16[128,16,32,32]{3,2,1,0:T(8,128)(2,1)} copy(bf16[128,16,32,32]{0,3,2,1:T(8,128)(2,1)} %fusion.17) | data formatting | bytes 8388608 | tf_op jit(solution)/shard_map/convert_element_type | solution.py:90
  348.2 23.3 %reshape.130 = bf16[2048,1024]{1,0:T(8,128)(2,1)} reshape(bf16[128,16,32,32]{3,2,1,0:T(8,128)(2,1)} %copy.106) | data formatting | bytes 8388608 | tf_op jit(solution)/shard_map/reshape | solution.py:90
  371.5 4.3 fusion.18
  375.8 1.2 copy.129
  380.7 51.4 %reduce-scatter.12.cloned.1.call-done = f32[16,64]{1,0:T(8,128)} async-done(((f32[256,64]{1,0:T(8,128)}), f32[16,64]{1,0:T(8,128)}) %reduce-scatter.12.cloned.1.call-update) | async-done | bytes 4112
  (192 shorter events, 17.5 us)
Async XLA Ops:
  7.2 37.6 %copy-start = (bf16[256,32]{0,1:T(8,128)(2,1)S(1)}, bf16[256,32]{0,1:T(8,128)(2,1)}, u32[]{:S(2)}) copy-start(bf16[256,32]{0,1:T(8,128)(2,1)} %param.24) | copy-start | bytes 49156
  7.2 368.6 %reduce-scatter.10.cloned.1.call-start = ((), (), s32[]{:S(2)}) async-start(), calls=%async_computation.4 | async-start | bytes 1114112
  8.1 36.6 %copy-start.29 = (f32[64,16]{1,0:T(8,128)}, f32[64,16]{1,0:T(8,128)S(1)}, u32[]{:S(2)}) copy-start(f32[64,16]{1,0:T(8,128)S(1)} %copy.101) | copy-start | bytes 12292
  9.1 37.1 %copy-start.31 = (f32[128,16]{0,1:T(8,128)}, f32[128,16]{0,1:T(8,128)S(1)}, u32[]{:S(2)}) copy-start(f32[128,16]{0,1:T(8,128)S(1)} %convolution_maximum_fusion) | copy-start | bytes 24580
  12.7 32.0 %copy-start.3 = (bf16[64,16,256]{2,1,0:T(8,128)(2,1)S(1)}, bf16[64,16,256]{2,1,0:T(8,128)(2,1)}, u32[]{:S(2)}) copy-start(bf16[64,16,256]{2,1,0:T(8,128)(2,1)} %param.16) | copy-start | bytes 1572868
  12.7 32.0 %copy-start.34 = (f32[256]{0:T(256)S(1)}, f32[256]{0:T(256)}, u32[]{:S(2)}) copy-start(f32[256]{0:T(256)} %param.21) | copy-start | bytes 3076
  12.7 32.1 %copy-start.36 = (f32[256]{0:T(256)S(1)}, f32[256]{0:T(256)}, u32[]{:S(2)}) copy-start(f32[256]{0:T(256)} %param.22) | copy-start | bytes 3076
  14.3 31.0 %copy-start.11 = (bf16[8,2048]{1,0:T(8,128)(2,1)}, bf16[8,2048]{1,0:T(8,128)(2,1)S(1)}, u32[]{:S(2)}) copy-start(bf16[8,2048]{1,0:T(8,128)(2,1)S(1)} %reshape.128) | copy-start | bytes 98308
  15.5 30.7 %copy-start.7 = (f32[64,16]{1,0:T(8,128)}, f32[64,16]{1,0:T(8,128)S(1)}, u32[]{:S(2)}) copy-start(f32[64,16]{1,0:T(8,128)S(1)} %broadcast_multiply_fusion.1) | copy-start | bytes 12292
  17.0 31.1 %copy-start.21 = (f32[64,16]{1,0:T(8,128)}, f32[64,16]{1,0:T(8,128)S(1)}, u32[]{:S(2)}) copy-start(f32[64,16]{1,0:T(8,128)S(1)} %fusion.26) | copy-start | bytes 12292
  17.0 31.1 %copy-start.6 = (bf16[128,16,128]{2,1,0:T(8,128)(2,1)S(1)}, bf16[128,16,128]{2,1,0:T(8,128)(2,1)}, u32[]{:S(2)}) copy-start(bf16[128,16,128]{2,1,0:T(8,128)(2,1)} %param.27) | copy-start | bytes 1572868
  17.0 31.0 %copy-start.19 = (f32[64,16]{1,0:T(8,128)}, f32[64,16]{1,0:T(8,128)S(1)}, u32[]{:S(2)}) copy-start(f32[64,16]{1,0:T(8,128)S(1)} %fusion.50) | copy-start | bytes 12292
  92.9 8.0 %copy-start.23 = (f32[64,16,32]{0,2,1:T(8,128)S(1)}, f32[64,16,32]{0,2,1:T(8,128)}, u32[]{:S(2)}) copy-start(f32[64,16,32]{0,2,1:T(8,128)} %get-tuple-element.247) | copy-start | bytes 393220 | tf_op jit(solution)/shard_map/while
  100.9 13.2 %copy-start.1 = (bf16[64,16,32,32]{3,2,1,0:T(8,128)(2,1)S(1)}, bf16[64,16,32,32]{3,2,1,0:T(8,128)(2,1)}, u32[]{:S(2)}) copy-start(bf16[64,16,32,32]{3,2,1,0:T(8,128)(2,1)} %reshape.157) | copy-start | bytes 6291460 | tf_op jit(solution)/shard_map/while
  174.9 8.0 %copy-start.23 = (f32[64,16,32]{0,2,1:T(8,128)S(1)}, f32[64,16,32]{0,2,1:T(8,128)}, u32[]{:S(2)}) copy-start(f32[64,16,32]{0,2,1:T(8,128)} %get-tuple-element.247) | copy-start | bytes 393220 | tf_op jit(solution)/shard_map/while
  182.9 13.2 %copy-start.1 = (bf16[64,16,32,32]{3,2,1,0:T(8,128)(2,1)S(1)}, bf16[64,16,32,32]{3,2,1,0:T(8,128)(2,1)}, u32[]{:S(2)}) copy-start(bf16[64,16,32,32]{3,2,1,0:T(8,128)(2,1)} %reshape.157) | copy-start | bytes 6291460 | tf_op jit(solution)/shard_map/while
  225.1 47.2 %copy-start.2 = (f32[1024,128]{1,0:T(8,128)}, f32[1024,128]{1,0:T(8,128)S(1)}, u32[]{:S(2)}) copy-start(f32[1024,128]{1,0:T(8,128)S(1)} %get-tuple-element.56) | copy-start | bytes 1572868
  225.1 47.3 %copy-start.25 = (f32[64,16,32]{0,2,1:T(8,128)S(1)}, f32[64,16,32]{0,2,1:T(8,128)}, u32[]{:S(2)}) copy-start(f32[64,16,32]{0,2,1:T(8,128)} %get-tuple-element.55) | copy-start | bytes 393220
  225.2 53.2 %copy-start.4 = (bf16[64,16,256]{2,1,0:T(8,128)(2,1)S(1)}, bf16[64,16,256]{2,1,0:T(8,128)(2,1)}, u32[]{:S(2)}) copy-start(bf16[64,16,256]{2,1,0:T(8,128)(2,1)} %param.16) | copy-start | bytes 1572868
  225.2 53.2 %copy-start.8 = (f32[64,16]{1,0:T(8,128)S(1)}, f32[64,16]{1,0:T(8,128)}, u32[]{:S(2)}) copy-start(f32[64,16]{1,0:T(8,128)} %copy-done.7) | copy-start | bytes 12292
  225.2 53.2 %copy-start.30 = (f32[64,16]{1,0:T(8,128)S(1)}, f32[64,16]{1,0:T(8,128)}, u32[]{:S(2)}) copy-start(f32[64,16]{1,0:T(8,128)} %copy-done.29) | copy-start | bytes 12292
  225.2 53.2 %copy-start.35 = (f32[256]{0:T(256)S(1)}, f32[256]{0:T(256)}, u32[]{:S(2)}) copy-start(f32[256]{0:T(256)} %param.21) | copy-start | bytes 3076
  225.2 59.3 %copy-start.22 = (f32[64,16]{1,0:T(8,128)S(1)}, f32[64,16]{1,0:T(8,128)}, u32[]{:S(2)}) copy-start(f32[64,16]{1,0:T(8,128)} %copy-done.21) | copy-start | bytes 12292
  225.2 65.3 %copy-start.20 = (f32[64,16]{1,0:T(8,128)S(1)}, f32[64,16]{1,0:T(8,128)}, u32[]{:S(2)}) copy-start(f32[64,16]{1,0:T(8,128)} %copy-done.19) | copy-start | bytes 12292
  229.4 79.2 %copy-start.37 = (f32[256]{0:T(256)S(1)}, f32[256]{0:T(256)}, u32[]{:S(2)}) copy-start(f32[256]{0:T(256)} %param.22) | copy-start | bytes 3076
  229.4 151.3 %reduce-scatter.8.cloned.1.call-start = ((), (), s32[]{:S(2)}) async-start(), calls=%async_computation.3 | async-start | bytes 557056 | tf_op jit(solution)/shard_map/reduce_scatter | solution.py:194
  229.5 6.1 %collective-permute-start = (bf16[8,2048]{1,0:T(8,128)(2,1)S(1)}, bf16[8,2048]{1,0:T(8,128)(2,1)S(1)}, u32[]{:S(2)}, u32[]{:S(2)}) collective-permute-start(bf16[8,2048]{1,0:T(8,128)(2,1)S(1)} %copy-done.12), channel_id=1, source_target_pairs={{0,1},{1,2},{2,3},{3,4},{4,5},{5,6},{6,7},{7,8},{8,9},{9,10},{10,1... | collective-permute-start | bytes 98312 | tf_op jit(solution)/shard_map/ppermute | solution.py:142
  235.6 6.0 %collective-permute-start.1 = (bf16[8,2048]{1,0:T(8,128)(2,1)S(1)}, bf16[8,2048]{1,0:T(8,128)(2,1)S(1)}, u32[]{:S(2)}, u32[]{:S(2)}) collective-permute-start(bf16[8,2048]{1,0:T(8,128)(2,1)S(1)} %collective-permute-done), channel_id=1, source_target_pairs={{0,1},{1,2},{2,3},{3,4},{4,5},{5,6},{6,7},{7,8},{8,9},{9,10},{10,1... | collective-permute-start | bytes 98312 | tf_op jit(solution)/shard_map/ppermute | solution.py:142
  241.6 6.0 %collective-permute-start.2 = (bf16[8,2048]{1,0:T(8,128)(2,1)S(1)}, bf16[8,2048]{1,0:T(8,128)(2,1)S(1)}, u32[]{:S(2)}, u32[]{:S(2)}) collective-permute-start(bf16[8,2048]{1,0:T(8,128)(2,1)S(1)} %collective-permute-done.1), channel_id=1, source_target_pairs={{0,1},{1,2},{2,3},{3,4},{4,5},{5,6},{6,7},{7,8},{8,9},{9,10},{10,1... | collective-permute-start | bytes 98312 | tf_op jit(solution)/shard_map/ppermute | solution.py:142
  247.7 6.0 %collective-permute-start.3 = (bf16[8,2048]{1,0:T(8,128)(2,1)S(1)}, bf16[8,2048]{1,0:T(8,128)(2,1)S(1)}, u32[]{:S(2)}, u32[]{:S(2)}) collective-permute-start(bf16[8,2048]{1,0:T(8,128)(2,1)S(1)} %collective-permute-done.2), channel_id=1, source_target_pairs={{0,1},{1,2},{2,3},{3,4},{4,5},{5,6},{6,7},{7,8},{8,9},{9,10},{10,1... | collective-permute-start | bytes 98312 | tf_op jit(solution)/shard_map/ppermute | solution.py:142
  253.7 6.4 %collective-permute-start.4 = (bf16[8,2048]{1,0:T(8,128)(2,1)S(1)}, bf16[8,2048]{1,0:T(8,128)(2,1)S(1)}, u32[]{:S(2)}, u32[]{:S(2)}) collective-permute-start(bf16[8,2048]{1,0:T(8,128)(2,1)S(1)} %collective-permute-done.3), channel_id=1, source_target_pairs={{0,1},{1,2},{2,3},{3,4},{4,5},{5,6},{6,7},{7,8},{8,9},{9,10},{10,1... | collective-permute-start | bytes 98312 | tf_op jit(solution)/shard_map/ppermute | solution.py:142
  260.1 6.2 %collective-permute-start.5 = (bf16[8,2048]{1,0:T(8,128)(2,1)S(1)}, bf16[8,2048]{1,0:T(8,128)(2,1)S(1)}, u32[]{:S(2)}, u32[]{:S(2)}) collective-permute-start(bf16[8,2048]{1,0:T(8,128)(2,1)S(1)} %collective-permute-done.4), channel_id=1, source_target_pairs={{0,1},{1,2},{2,3},{3,4},{4,5},{5,6},{6,7},{7,8},{8,9},{9,10},{10,1... | collective-permute-start | bytes 98312 | tf_op jit(solution)/shard_map/ppermute | solution.py:142
  266.3 6.0 %collective-permute-start.6 = (bf16[8,2048]{1,0:T(8,128)(2,1)S(1)}, bf16[8,2048]{1,0:T(8,128)(2,1)S(1)}, u32[]{:S(2)}, u32[]{:S(2)}) collective-permute-start(bf16[8,2048]{1,0:T(8,128)(2,1)S(1)} %collective-permute-done.5), channel_id=1, source_target_pairs={{0,1},{1,2},{2,3},{3,4},{4,5},{5,6},{6,7},{7,8},{8,9},{9,10},{10,1... | collective-permute-start | bytes 98312 | tf_op jit(solution)/shard_map/ppermute | solution.py:142
  272.3 6.0 %collective-permute-start.7 = (bf16[8,2048]{1,0:T(8,128)(2,1)S(1)}, bf16[8,2048]{1,0:T(8,128)(2,1)S(1)}, u32[]{:S(2)}, u32[]{:S(2)}) collective-permute-start(bf16[8,2048]{1,0:T(8,128)(2,1)S(1)} %collective-permute-done.6), channel_id=1, source_target_pairs={{0,1},{1,2},{2,3},{3,4},{4,5},{5,6},{6,7},{7,8},{8,9},{9,10},{10,1... | collective-permute-start | bytes 98312 | tf_op jit(solution)/shard_map/ppermute | solution.py:142
  272.4 159.7 %reduce-scatter.12.cloned.1.call-start = ((), (), s32[]{:S(2)}) async-start(), calls=%async_computation.5 | async-start | bytes 139264
  272.7 42.0 %copy-start.14 = (f32[64,128]{1,0:T(8,128)S(1)}, f32[64,128]{1,0:T(8,128)}, u32[]{:S(2)}) copy-start(f32[64,128]{1,0:T(8,128)} %copy-done.13) | copy-start | bytes 98308
  278.4 6.1 %collective-permute-start.8 = (bf16[8,2048]{1,0:T(8,128)(2,1)S(1)}, bf16[8,2048]{1,0:T(8,128)(2,1)S(1)}, u32[]{:S(2)}, u32[]{:S(2)}) collective-permute-start(bf16[8,2048]{1,0:T(8,128)(2,1)S(1)} %collective-permute-done.7), channel_id=1, source_target_pairs={{0,1},{1,2},{2,3},{3,4},{4,5},{5,6},{6,7},{7,8},{8,9},{9,10},{10,1... | collective-permute-start | bytes 98312 | tf_op jit(solution)/shard_map/ppermute | solution.py:142
  284.5 6.0 %collective-permute-start.9 = (bf16[8,2048]{1,0:T(8,128)(2,1)S(1)}, bf16[8,2048]{1,0:T(8,128)(2,1)S(1)}, u32[]{:S(2)}, u32[]{:S(2)}) collective-permute-start(bf16[8,2048]{1,0:T(8,128)(2,1)S(1)} %collective-permute-done.8), channel_id=1, source_target_pairs={{0,1},{1,2},{2,3},{3,4},{4,5},{5,6},{6,7},{7,8},{8,9},{9,10},{10,1... | collective-permute-start | bytes 98312 | tf_op jit(solution)/shard_map/ppermute | solution.py:142
  290.5 6.0 %collective-permute-start.10 = (bf16[8,2048]{1,0:T(8,128)(2,1)S(1)}, bf16[8,2048]{1,0:T(8,128)(2,1)S(1)}, u32[]{:S(2)}, u32[]{:S(2)}) collective-permute-start(bf16[8,2048]{1,0:T(8,128)(2,1)S(1)} %collective-permute-done.9), channel_id=1, source_target_pairs={{0,1},{1,2},{2,3},{3,4},{4,5},{5,6},{6,7},{7,8},{8,9},{9,10},{10,1... | collective-permute-start | bytes 98312 | tf_op jit(solution)/shard_map/ppermute | solution.py:142
  296.6 6.0 %collective-permute-start.11 = (bf16[8,2048]{1,0:T(8,128)(2,1)S(1)}, bf16[8,2048]{1,0:T(8,128)(2,1)S(1)}, u32[]{:S(2)}, u32[]{:S(2)}) collective-permute-start(bf16[8,2048]{1,0:T(8,128)(2,1)S(1)} %collective-permute-done.10), channel_id=1, source_target_pairs={{0,1},{1,2},{2,3},{3,4},{4,5},{5,6},{6,7},{7,8},{8,9},{9,10},{10,1... | collective-permute-start | bytes 98312 | tf_op jit(solution)/shard_map/ppermute | solution.py:142
  296.6 25.2 %copy-start.27 = (bf16[64,16,32]{2,1,0:T(8,128)(2,1)S(1)}, bf16[64,16,32]{2,1,0:T(8,128)(2,1)}, u32[]{:S(2)}) copy-start(bf16[64,16,32]{2,1,0:T(8,128)(2,1)} %copy-done.26) | copy-start | bytes 196612
  296.6 25.2 %copy-start.32 = (f32[128,16]{0,1:T(8,128)S(1)}, f32[128,16]{0,1:T(8,128)}, u32[]{:S(2)}) copy-start(f32[128,16]{0,1:T(8,128)} %copy-done.31) | copy-start | bytes 24580
  302.6 6.0 %collective-permute-start.12 = (bf16[8,2048]{1,0:T(8,128)(2,1)S(1)}, bf16[8,2048]{1,0:T(8,128)(2,1)S(1)}, u32[]{:S(2)}, u32[]{:S(2)}) collective-permute-start(bf16[8,2048]{1,0:T(8,128)(2,1)S(1)} %collective-permute-done.11), channel_id=1, source_target_pairs={{0,1},{1,2},{2,3},{3,4},{4,5},{5,6},{6,7},{7,8},{8,9},{9,10},{10,1... | collective-permute-start | bytes 98312 | tf_op jit(solution)/shard_map/ppermute | solution.py:142
  308.6 6.0 %collective-permute-start.13 = (bf16[8,2048]{1,0:T(8,128)(2,1)S(1)}, bf16[8,2048]{1,0:T(8,128)(2,1)S(1)}, u32[]{:S(2)}, u32[]{:S(2)}) collective-permute-start(bf16[8,2048]{1,0:T(8,128)(2,1)S(1)} %collective-permute-done.12), channel_id=1, source_target_pairs={{0,1},{1,2},{2,3},{3,4},{4,5},{5,6},{6,7},{7,8},{8,9},{9,10},{10,1... | collective-permute-start | bytes 98312 | tf_op jit(solution)/shard_map/ppermute | solution.py:142
  314.7 6.4 %collective-permute-start.14 = (bf16[8,2048]{1,0:T(8,128)(2,1)S(1)}, bf16[8,2048]{1,0:T(8,128)(2,1)S(1)}, u32[]{:S(2)}, u32[]{:S(2)}) collective-permute-start(bf16[8,2048]{1,0:T(8,128)(2,1)S(1)} %collective-permute-done.13), channel_id=1, source_target_pairs={{0,1},{1,2},{2,3},{3,4},{4,5},{5,6},{6,7},{7,8},{8,9},{9,10},{10,1... | collective-permute-start | bytes 98312 | tf_op jit(solution)/shard_map/ppermute | solution.py:142
  348.2 23.3 %copy-start.28 = (bf16[1024,128]{1,0:T(8,128)(2,1)S(1)}, bf16[1024,128]{1,0:T(8,128)(2,1)}, u32[]{:S(2)}) copy-start(bf16[1024,128]{1,0:T(8,128)(2,1)} %param.25) | copy-start | bytes 786436
  348.2 23.3 %copy-start.38 = (f32[128]{0:T(128)S(1)}, f32[128]{0:T(128)}, u32[]{:S(2)}) copy-start(f32[128]{0:T(128)} %param.26) | copy-start | bytes 1540
  371.5 7.7 %copy-start.18 = (f32[64,8]{1,0:T(8,128)S(1)}, f32[64,8]{1,0:T(8,128)}, u32[]{:S(2)}) copy-start(f32[64,8]{1,0:T(8,128)} %copy-done.17) | copy-start | bytes 6148
  (12 other events, 49.3 us)
Sparse Core Ops, SparseCore 0:
  229.6 55.0 reduce-scatter.9
  289.2 54.8 reduce-scatter.7
  379.8 52.2 reduce-scatter.11
